TPU v7x, 32 devices: a whole 2x2x4 slice. The times are simulated.
32 devices in a mesh: seq: 8 (over y, x, core), head: 4 (over z).
Axes of the slice: x: 2, y: 2, z: 4, core: 2. Of those that a mesh axis runs over, the one named last changes fastest.
Arguments:
- tokens: bfloat16 [24576, 768], P(('seq', 'head')), may hold values from -6 to 6
- cotangent: bfloat16 [24576, 768], P(('seq', 'head')), may hold values from -6 to 6
- lengths: int32 [8, 24], P('seq'), may hold values from 1 to 512, 3072 in all within a row
- labels: int32 [8, 24], P('seq'), may hold values from 0 to 2
- w_qkv: bfloat16 [768, 2304], replicated, may hold values from -0.3125 to 0.3125
- b_query: float32 [768], replicated, may hold values from -3 to 3
- b_value: float32 [768], replicated, may hold values from -3 to 3
- w_out: bfloat16 [768, 768], replicated, may hold values from -0.625 to 0.625
- b_out: float32 [768], replicated, may hold values from -3 to 3
- gain_attn: float32 [768], replicated, may hold values from 0.1 to 1.9
- shift_attn: float32 [768], replicated, may hold values from -3 to 3
- w_in: bfloat16 [768, 3072], replicated, may hold values from -0.21875 to 0.21875
- b_in: float32 [3072], replicated, may hold values from -3 to 3
- w_back: bfloat16 [3072, 768], replicated, may hold values from -0.15625 to 0.15625
- b_back: float32 [768], replicated, may hold values from -3 to 3
- gain_ffn: float32 [768], replicated, may hold values from 0.1 to 1.9
- shift_ffn: float32 [768], replicated, may hold values from -3 to 3
- w_pool: bfloat16 [768, 768], replicated, may hold values from -0.21875 to 0.21875
- b_pool: float32 [768], replicated, may hold values from -3 to 3
- w_class: float32 [768, 3], replicated, may hold values from -0.625 to 0.625
Outputs:
- output: bfloat16 [24576, 768], P(('seq', 'head'))
- grad_tokens: float32 [24576, 768], P(('seq', 'head'))
- grad_w_qkv: float32 [768, 2304], P(('seq', 'head'))
- grad_b_query: float32 [768], P(('seq', 'head'))
- grad_b_value: float32 [768], P(('seq', 'head'))
- grad_w_out: float32 [768, 768], P(('seq', 'head'))
- grad_b_out: float32 [768], P(('seq', 'head'))
- grad_gain_attn: float32 [768], P(('seq', 'head'))
- grad_shift_attn: float32 [768], P(('seq', 'head'))
- grad_w_in: float32 [768, 3072], P(('seq', 'head'))
- grad_b_in: float32 [3072], P(('seq', 'head'))
- grad_w_back: float32 [3072, 768], P(('seq', 'head'))
- grad_b_back: float32 [768], P(('seq', 'head'))
- grad_gain_ffn: float32 [768], P(('seq', 'head'))
- grad_shift_ffn: float32 [768], P(('seq', 'head'))
- grad_w_pool: float32 [768, 768], P(('seq', 'head'))
- grad_b_pool: float32 [768], P(('seq', 'head'))
- grad_w_class: float32 [768, 3], P(('seq', 'head'))
- entropy: float32 [], replicated
Inputs may be any that keep to these rules, and one draw needn't show every extreme that they name: Each row of 24 lengths sums to 3072, and its largest length is 512.
All inputs are finite; a program needn't handle non-finite values.
Results may differ from a plain program's by a relative error of at most 0.014.
The roundings to bfloat16 on the way count: a program that leaves them out, or rounds other values in their place, can miss the bound.
Values may be sent and summed in bfloat16 or wider, within the bound.
A program may use at most 192 MiB of HBM per device.

v0:
```python
import jax
import jax.numpy as jnp
from jax import lax
from jax.sharding import PartitionSpec as P

HEAD_DIM = 64
MAXLEN = 512
eps = 1e-05
big_neg = -1e30
highest = lax.Precision.HIGHEST


def exact_gelu(values):
    return jax.nn.gelu(values, approximate=False)


def layer_norm(hidden, gain_vec, shift_vec):
    centred = hidden - jnp.mean(hidden, axis=-1, keepdims=True)
    inv_std = lax.rsqrt(jnp.mean(centred * centred, axis=-1, keepdims=True) + eps)
    normed = centred * inv_std
    return (normed * gain_vec + shift_vec, normed, inv_std)


def norm_back(grad_out, normed, inv_std, gain_vec):
    grad_norm = grad_out * gain_vec
    inner = grad_norm - jnp.mean(grad_norm, axis=-1, keepdims=True)
    inner = inner - normed * jnp.mean(grad_norm * normed, axis=-1, keepdims=True)
    return (inv_std * inner, jnp.sum(grad_out * normed, axis=0), jnp.sum(grad_out, axis=0))


def block_scores(q_block, k_window, seg_query, seg_key):
    raw_scores = jnp.einsum(
        "hdq,hdk->hqk", q_block, k_window, preferred_element_type=jnp.float32
    ) * HEAD_DIM ** (-0.5)
    same_seq = seg_query[:, None] == seg_key[None, :]
    return jnp.where(same_seq[None], raw_scores, big_neg)


def pad_keys(k_heads, v_heads, seg_all, block_len):
    padding = ((0, 0), (0, 0), (block_len, block_len))
    return (
        jnp.pad(k_heads, padding),
        jnp.pad(v_heads, padding),
        jnp.pad(seg_all, (block_len, block_len), constant_values=-1),
    )


def attend_forward(q_heads, k_heads, v_heads, seg_all, block_len):
    local_heads, head_width, group_rows = q_heads.shape
    k_padded, v_padded, seg_padded = pad_keys(k_heads, v_heads, seg_all, block_len)

    def one_block(block_index):
        offset = block_index * block_len
        q_block = lax.dynamic_slice_in_dim(q_heads, offset, block_len, 2)
        k_window = lax.dynamic_slice_in_dim(k_padded, offset, 3 * block_len, 2)
        v_window = lax.dynamic_slice_in_dim(v_padded, offset, 3 * block_len, 2)
        seg_query = lax.dynamic_slice_in_dim(seg_all, offset, block_len, 0)
        seg_key = lax.dynamic_slice_in_dim(seg_padded, offset, 3 * block_len, 0)
        scores = block_scores(q_block, k_window, seg_query, seg_key)
        row_peak = jnp.max(scores, axis=-1, keepdims=True)
        expo = jnp.exp(scores - row_peak)
        row_total = jnp.sum(expo, axis=-1, keepdims=True)
        weights_low = (expo / row_total).astype(jnp.bfloat16)
        context_block = jnp.einsum(
            "hdk,hqk->hdq", v_window, weights_low, preferred_element_type=jnp.float32
        )
        return (context_block, (row_peak + jnp.log(row_total))[..., 0])

    context_blocks, log_norm = lax.map(
        one_block, jnp.arange(group_rows // block_len, dtype=jnp.int32)
    )
    context = jnp.transpose(context_blocks, (1, 2, 0, 3)).reshape(
        local_heads * head_width, group_rows
    )
    return (context, log_norm)


def attend_backward(q_heads, k_heads, v_heads, grad_ctx, seg_all, log_norm, block_len):
    local_heads, head_width, group_rows = q_heads.shape
    k_padded, v_padded, seg_padded = pad_keys(k_heads, v_heads, seg_all, block_len)

    def one_block(carry, inputs):
        grad_keys, grad_values = carry
        block_index, block_norm = inputs
        offset = block_index * block_len
        q_block = lax.dynamic_slice_in_dim(q_heads, offset, block_len, 2)
        k_window = lax.dynamic_slice_in_dim(k_padded, offset, 3 * block_len, 2)
        v_window = lax.dynamic_slice_in_dim(v_padded, offset, 3 * block_len, 2)
        grad_block = lax.dynamic_slice_in_dim(grad_ctx, offset, block_len, 2)
        seg_query = lax.dynamic_slice_in_dim(seg_all, offset, block_len, 0)
        seg_key = lax.dynamic_slice_in_dim(seg_padded, offset, 3 * block_len, 0)
        scores = block_scores(q_block, k_window, seg_query, seg_key)
        weights = jnp.exp(scores - block_norm[..., None])
        weights_low = weights.astype(jnp.bfloat16)
        grad_weights = jnp.einsum(
            "hdq,hdk->hqk", grad_block, v_window, preferred_element_type=jnp.float32
        )
        row_dot = jnp.sum(weights * grad_weights, axis=-1, keepdims=True)
        grad_scores = (weights * (grad_weights - row_dot) * HEAD_DIM ** (-0.5)).astype(jnp.bfloat16)
        grad_query = jnp.einsum(
            "hqk,hdk->hdq", grad_scores, k_window, preferred_element_type=jnp.float32
        )
        key_part = jnp.einsum(
            "hqk,hdq->hdk", grad_scores, q_block, preferred_element_type=jnp.float32
        )
        value_part = jnp.einsum(
            "hqk,hdq->hdk", weights_low, grad_block, preferred_element_type=jnp.float32
        )
        grad_keys = lax.dynamic_update_slice_in_dim(
            grad_keys,
            lax.dynamic_slice_in_dim(grad_keys, offset, 3 * block_len, 2) + key_part,
            offset,
            2,
        )
        grad_values = lax.dynamic_update_slice_in_dim(
            grad_values,
            lax.dynamic_slice_in_dim(grad_values, offset, 3 * block_len, 2) + value_part,
            offset,
            2,
        )
        return ((grad_keys, grad_values), grad_query)

    zero_pad = jnp.zeros(k_padded.shape, jnp.float32)
    block_ids = jnp.arange(group_rows // block_len, dtype=jnp.int32)
    (grad_keys, grad_values), grad_queries = lax.scan(
        one_block, (zero_pad, zero_pad), (block_ids, log_norm)
    )
    grad_q = jnp.transpose(grad_queries, (1, 2, 0, 3)).reshape(local_heads * head_width, group_rows)
    grad_k = grad_keys[:, :, block_len : block_len + group_rows].reshape(
        local_heads * head_width, group_rows
    )
    grad_v = grad_values[:, :, block_len : block_len + group_rows].reshape(
        local_heads * head_width, group_rows
    )
    return (grad_q, grad_k, grad_v)


def local(
    tokens,
    cotangent,
    lengths,
    labels,
    w_qkv,
    b_query,
    b_value,
    w_out,
    b_out,
    gain_attn,
    shift_attn,
    w_in,
    b_in,
    w_back,
    b_back,
    gain_ffn,
    shift_ffn,
    w_pool,
    b_pool,
    w_class,
):
    n_head = lax.axis_size("head")
    n_seq = lax.axis_size("seq")
    head_index = lax.axis_index("head")
    tok_rows, model_width = tokens.shape
    group_rows = tok_rows * n_head
    block_len = MAXLEN
    local_width = model_width // n_head
    local_heads = local_width // HEAD_DIM
    contract_first = (((0,), (0,)), ((), ()))
    contract_last = (((1,), (1,)), ((), ()))
    seq_lengths = lengths[0]
    starts = jnp.cumsum(seq_lengths) - seq_lengths
    group_pos = jnp.arange(group_rows, dtype=jnp.int32)
    seg_all = jnp.sum((starts[None, :] <= group_pos[:, None]).astype(jnp.int32), axis=1) - 1
    qkv_cols = lax.dot_general(
        w_qkv, tokens, (((0,), (1,)), ((), ())), preferred_element_type=jnp.float32
    )
    bias_cols = jnp.concatenate([b_query, jnp.zeros_like(b_query), b_value])[:, None]
    qkv_low = (qkv_cols + bias_cols).astype(jnp.bfloat16).reshape(3, model_width, tok_rows)
    qkv_heads = lax.all_to_all(qkv_low, "head", split_axis=1, concat_axis=2, tiled=True)
    q_heads = qkv_heads[0].reshape(local_heads, HEAD_DIM, group_rows)
    k_heads = qkv_heads[1].reshape(local_heads, HEAD_DIM, group_rows)
    v_heads = qkv_heads[2].reshape(local_heads, HEAD_DIM, group_rows)
    context, log_norm = attend_forward(q_heads, k_heads, v_heads, seg_all, block_len)
    context_cols = lax.all_to_all(
        context.astype(jnp.bfloat16), "head", split_axis=1, concat_axis=0, tiled=True
    )
    attn_out = (
        lax.dot_general(context_cols, w_out, contract_first, preferred_element_type=jnp.float32)
        + b_out
    )
    normed_attn, unit_attn, inv_attn = layer_norm(
        tokens.astype(jnp.float32) + attn_out, gain_attn, shift_attn
    )
    middle = normed_attn.astype(jnp.bfloat16)
    pre_act = jnp.dot(middle, w_in, preferred_element_type=jnp.float32) + b_in
    activated_f32, gelu_pull = jax.vjp(exact_gelu, pre_act)
    activated = activated_f32.astype(jnp.bfloat16)
    ffn_out = jnp.dot(activated, w_back, preferred_element_type=jnp.float32) + b_back
    normed_ffn, unit_ffn, inv_ffn = layer_norm(
        middle.astype(jnp.float32) + ffn_out, gain_ffn, shift_ffn
    )
    output = normed_ffn.astype(jnp.bfloat16)
    row_base = head_index * tok_rows
    my_rows = row_base + jnp.arange(tok_rows, dtype=jnp.int32)
    my_seg = lax.dynamic_slice_in_dim(seg_all, row_base, tok_rows, 0)
    is_start = jnp.take(starts, my_seg) == my_rows
    owner_sel = (starts[:, None] == my_rows[None, :]).astype(jnp.bfloat16)
    owned = jnp.sum(owner_sel.astype(jnp.float32), axis=1)
    cls_low = jnp.dot(owner_sel, output, preferred_element_type=jnp.float32).astype(jnp.bfloat16)
    pooled = jnp.tanh(jnp.dot(cls_low, w_pool, preferred_element_type=jnp.float32) + b_pool)
    logits = jnp.dot(pooled, w_class, precision=highest)
    class_peak = jnp.max(logits, axis=-1, keepdims=True)
    class_exp = jnp.exp(logits - class_peak)
    class_total = jnp.sum(class_exp, axis=-1, keepdims=True)
    class_probs = class_exp / class_total
    ramp_norm = (class_peak + jnp.log(class_total))[:, 0]
    entropy_terms = owned * (ramp_norm - jnp.sum(class_probs * logits, axis=-1))
    entropy_all = lax.psum(jnp.sum(entropy_terms), ("seq", "head"))
    entropy_mean = entropy_all / (n_seq * labels.shape[1])
    onehot = (labels[0][:, None] == jnp.arange(w_class.shape[1], dtype=jnp.int32)[None, :]).astype(
        jnp.float32
    )
    grad_logits = (class_probs - onehot) * owned[:, None]
    grad_class = lax.dot_general(pooled, grad_logits, contract_first, precision=highest)
    grad_pooled = lax.dot_general(grad_logits, w_class, contract_last, precision=highest)
    grad_pre_pool = (grad_pooled * (1.0 - pooled * pooled)).astype(jnp.bfloat16)
    grad_pool = lax.dot_general(
        cls_low, grad_pre_pool, contract_first, preferred_element_type=jnp.float32
    )
    grad_bpool = jnp.sum(grad_pre_pool.astype(jnp.float32), axis=0)
    grad_cls = lax.dot_general(
        grad_pre_pool, w_pool, contract_last, preferred_element_type=jnp.float32
    )
    cls_back = jnp.where(is_start[:, None], jnp.take(grad_cls, my_seg, axis=0), 0.0)
    grad_result = cotangent.astype(jnp.float32) + cls_back
    grad_ffn_res, grad_gain_ffn, grad_shift_ffn = norm_back(
        grad_result, unit_ffn, inv_ffn, gain_ffn
    )
    grad_ffn = grad_ffn_res.astype(jnp.bfloat16)
    grad_wback = lax.dot_general(
        activated, grad_ffn, contract_first, preferred_element_type=jnp.float32
    )
    grad_bback = jnp.sum(grad_ffn.astype(jnp.float32), axis=0)
    grad_act = lax.dot_general(grad_ffn, w_back, contract_last, preferred_element_type=jnp.float32)
    grad_pre = gelu_pull(grad_act)[0].astype(jnp.bfloat16)
    grad_win = lax.dot_general(middle, grad_pre, contract_first, preferred_element_type=jnp.float32)
    grad_bin = jnp.sum(grad_pre.astype(jnp.float32), axis=0)
    grad_middle = grad_ffn_res + lax.dot_general(
        grad_pre, w_in, contract_last, preferred_element_type=jnp.float32
    )
    grad_attn_res, grad_gain_attn, grad_shift_attn = norm_back(
        grad_middle, unit_attn, inv_attn, gain_attn
    )
    grad_attn = grad_attn_res.astype(jnp.bfloat16)
    grad_wout = lax.dot_general(
        context_cols, grad_attn, (((1,), (0,)), ((), ())), preferred_element_type=jnp.float32
    )
    grad_bout = jnp.sum(grad_attn.astype(jnp.float32), axis=0)
    grad_ctx_cols = lax.dot_general(
        w_out, grad_attn, contract_last, preferred_element_type=jnp.float32
    )
    grad_ctx_heads = lax.all_to_all(
        grad_ctx_cols.astype(jnp.bfloat16), "head", split_axis=0, concat_axis=1, tiled=True
    )
    grad_q, grad_k, grad_v = attend_backward(
        q_heads,
        k_heads,
        v_heads,
        grad_ctx_heads.reshape(local_heads, HEAD_DIM, group_rows),
        seg_all,
        log_norm,
        block_len,
    )
    grad_stack = jnp.stack([grad_q, grad_k, grad_v]).astype(jnp.bfloat16)
    grad_qkv = lax.all_to_all(grad_stack, "head", split_axis=2, concat_axis=1, tiled=True).reshape(
        3 * model_width, tok_rows
    )
    grad_tokens = grad_attn_res + lax.dot_general(
        grad_qkv, w_qkv, (((0,), (1,)), ((), ())), preferred_element_type=jnp.float32
    )
    grad_wqkv = lax.dot_general(
        tokens, grad_qkv, (((0,), (1,)), ((), ())), preferred_element_type=jnp.float32
    )
    grad_bquery = jnp.sum(grad_qkv[:model_width].astype(jnp.float32), axis=1)
    grad_bvalue = jnp.sum(grad_qkv[2 * model_width :].astype(jnp.float32), axis=1)
    summed = (
        lax.psum_scatter(grad_wqkv, ("seq", "head"), scatter_dimension=0, tiled=True),
        lax.psum_scatter(grad_bquery, ("seq", "head"), scatter_dimension=0, tiled=True),
        lax.psum_scatter(grad_bvalue, ("seq", "head"), scatter_dimension=0, tiled=True),
        lax.psum_scatter(grad_wout, ("seq", "head"), scatter_dimension=0, tiled=True),
        lax.psum_scatter(grad_bout, ("seq", "head"), scatter_dimension=0, tiled=True),
        lax.psum_scatter(grad_gain_attn, ("seq", "head"), scatter_dimension=0, tiled=True),
        lax.psum_scatter(grad_shift_attn, ("seq", "head"), scatter_dimension=0, tiled=True),
        lax.psum_scatter(grad_win, ("seq", "head"), scatter_dimension=0, tiled=True),
        lax.psum_scatter(grad_bin, ("seq", "head"), scatter_dimension=0, tiled=True),
        lax.psum_scatter(grad_wback, ("seq", "head"), scatter_dimension=0, tiled=True),
        lax.psum_scatter(grad_bback, ("seq", "head"), scatter_dimension=0, tiled=True),
        lax.psum_scatter(grad_gain_ffn, ("seq", "head"), scatter_dimension=0, tiled=True),
        lax.psum_scatter(grad_shift_ffn, ("seq", "head"), scatter_dimension=0, tiled=True),
        lax.psum_scatter(grad_pool, ("seq", "head"), scatter_dimension=0, tiled=True),
        lax.psum_scatter(grad_bpool, ("seq", "head"), scatter_dimension=0, tiled=True),
        lax.psum_scatter(grad_class, ("seq", "head"), scatter_dimension=0, tiled=True),
    )
    return (
        output,
        grad_tokens,
        summed[0],
        summed[1],
        summed[2],
        summed[3],
        summed[4],
        summed[5],
        summed[6],
        summed[7],
        summed[8],
        summed[9],
        summed[10],
        summed[11],
        summed[12],
        summed[13],
        summed[14],
        summed[15],
        entropy_mean,
    )


def solution(mesh):
    placed = (
        P(("seq", "head"), None),
        P(("seq", "head"), None),
        P("seq", None),
        P("seq", None),
        P(),
        P(),
        P(),
        P(),
        P(),
        P(),
        P(),
        P(),
        P(),
        P(),
        P(),
        P(),
        P(),
        P(),
        P(),
        P(),
    )
    return jax.shard_map(
        local,
        mesh=mesh,
        in_specs=placed,
        out_specs=(
            P(("seq", "head"), None),
            P(("seq", "head"), None),
            P(("seq", "head"), None),
            P(("seq", "head")),
            P(("seq", "head")),
            P(("seq", "head"), None),
            P(("seq", "head")),
            P(("seq", "head")),
            P(("seq", "head")),
            P(("seq", "head"), None),
            P(("seq", "head")),
            P(("seq", "head"), None),
            P(("seq", "head")),
            P(("seq", "head")),
            P(("seq", "head")),
            P(("seq", "head"), None),
            P(("seq", "head")),
            P(("seq", "head"), None),
            P(),
        ),
        check_vma=False,
    )
```

profile of v0, /device:TPU:0, one launch (start us, length us, event | category | flops | bytes accessed | tf_op | source)
XLA Modules:
  0.0 1120.1 jit_solution(16411158388768672741)
XLA Ops:
  9.2 5.1 add_convert_fusion.1
  14.3 5.2 copy.152
  19.5 6.7 all-to-all-start
  29.1 101.8 %all-to-all-done = bf16[3,768,768]{2,0,1:T(4,128)(2,1)} async-done(((bf16[3,768,768]{2,0,1:T(4,128)(2,1)}), bf16[3,768,768]{2,0,1:T(4,128)(2,1)}, u32[]{:S(2)}, u32[]{:S(2)}) %all-to-all-start) | async-done | bytes 3538976 | tf_op jit(solution)/shard_map/all_to_all | solution.py:179
  130.9 11.1 fusion.92
  167.8 88.9 %while.26 = (s32[]{:T(128)}, bf16[6,3,64,512]{3,2,1,0:T(8,128)(2,1)}, f32[6,3,512]{2,1,0:T(4,128)}, s32[6]{0:T(128)S(1)}, bf16[3,64,4096]{2,1,0:T(8,128)(2,1)}, ...) while((s32[]{:T(128)}, ...), condition=%wide.region_5.6_spmd, body=%wide.region_2.5_spmd.sunk | while | flops 633076224 | bytes 33304036 | solution.py:69
  177.9 4.8 fusion.151
  192.7 4.8 fusion.151
  207.5 4.8 fusion.151
  222.3 4.8 fusion.151
  237.1 4.8 fusion.151
  251.9 4.8 fusion.151
  266.0 4.4 all-to-all-start.1
  276.5 16.7 %fusion.71 = (pred[768]{0:T(1024)(128)(4,1)}, s32[768]{0:T(1024)S(1)}) fusion(s32[]{:T(128)} %bitcast.16, s32[]{:T(128)} %bitcast.17, s32[]{:T(128)} %bitcast.18, s32[]{:T(128)} %bitcast.19, s32[]{:T(128)} %bitcast.20, s32[]{:T(128)} %bitcast.21, s32[]{:T(128)} %bitcast.22, s32[]{:T(128)} %bitcast.23, s32[]{:T(128)} %bitcast.24, s32[]{:T(128)} %bitcast.25, ...), kind=kLoop, calls=%fused_computation.120 | loop fusion | flops 42240 | bytes 7016 | tf_op jit(solution)/shard_map/eq | solution.py:206
  302.3 30.3 %multiply_convert_fusion.1 = (bf16[768,3072]{1,0:T(8,128)(2,1)S(1)}, f32[768,3072]{1,0:T(8,128)}, f32[768,3072]{1,0:T(8,128)}) fusion(f32[3072]{0:T(1024)S(1)} %copy-done.38, bf16[768,3072]{1,0:T(8,128)(2,1)} %param.35, f32[768,768]{0,1:T(8,128)S(1)} %get-tuple-element.372, f32[768]{0:T(1024)S(1)} %copy-done.42, f32[768]{0:T(1024)S(1)} %copy-done.33, ...), kind=kOutput, calls=%fused_computation.57 | convolution fusion | flops 3782541312 | bytes 30695424 | tf_op jit(solution)/shard_map/dot_general | solution.py:195
  332.6 4.8 fusion.96
  344.5 5.0 gather_fusion
  352.6 4.6 multiply_reduce_fusion.1
  358.8 15.4 %convert_reduce_fusion = (f32[3072]{0:T(1024)}, bf16[768,3072]{1,0:T(8,128)(2,1)}) fusion(f32[768,3072]{1,0:T(8,128)} %get-tuple-element.341, bf16[3072,768]{1,0:T(8,128)(2,1)} %param.37, f32[768,768]{0,1:T(8,128)S(1)} %get-tuple-element.334, f32[768,3072]{1,0:T(8,128)} %get-tuple-element.373, f32[3072]{0:T(1024)S(1)} %copy-done.39), kind=kOutput, calls=%fused_computation.55 | convolution fusion | flops 3664573440 | bytes 30695424 | tf_op jit(solution)/shard_map/dot_general | solution.py:244
  374.3 7.5 multiply_reduce_fusion.2
  389.0 10.6 fusion.98
  403.9 4.3 all-to-all-start.2
  408.2 10.8 fusion.83
  419.1 22.6 %all-to-all-done.2 = bf16[4,192,768]{2,1,0:T(8,128)(2,1)} async-done(((bf16[4,192,768]{2,1,0:T(8,128)(2,1)}), bf16[4,192,768]{2,1,0:T(8,128)(2,1)}, u32[]{:S(2)}, u32[]{:S(2)}) %all-to-all-start.2) | async-done | bytes 1179680 | tf_op jit(solution)/shard_map/all_to_all | solution.py:262
  453.6 333.4 %while.27 = (s32[]{:T(128)}, f32[3,64,4096]{2,1,0:T(8,128)}, f32[3,64,4096]{2,1,0:T(8,128)}, bf16[6,3,64,512]{3,2,1,0:T(8,128)(2,1)}, s32[6]{0:T(128)S(1)}, /*in...) while((s32[]{:T(128)}, f32[3,64,4096]{2,1,0:T(8,128)}, ...), condition=%wide.region_19.20_spmd, body=%wide.region_17.19_spmd.sunk | while | flops 1544361984 | bytes 113093408 | solution.py:125
  457.6 7.3 subtract_exponential_fusion.4
  464.9 6.2 fusion.162
  471.1 15.8 %fusion.163 = f32[3,64,4096]{2,1,0:T(8,128)} fusion(f32[3,64,4096]{2,1,0:T(8,128)} %get-tuple-element.577, s32[]{:T(128)S(6)} %select_n.97, f32[3,512,1536]{2,1,0:T(8,128)} %subtract_exponential_fusion.4, f32[3,512,1536]{2,1,0:T(8,128)} %fusion.162, bf16[3,64,3072]{2,1,0:T(8,128)(2,1)} %get-tuple-element.598, s32[]{:T(128)S(6)} %select_n.98), kind=kOutput, calls=%fused_computation.31.clone.1 | convolution fusion | flops 314084352 | bytes 40304648 | tf_op jit(solution)/shard_map/while/body/eval_jaxpr/hqk,hdq->hdk/dot_general | solution.py:103
  487.0 15.5 %fusion.165 = bf16[6,3,64,512]{3,2,1,0:T(8,128)(2,1)} fusion(bf16[6,3,64,512]{3,2,1,0:T(8,128)(2,1)} %get-tuple-element.579, s32[]{:T(128)} %get-tuple-element.576, f32[3,512,1536]{2,1,0:T(8,128)} %subtract_exponential_fusion.4, f32[3,512,1536]{2,1,0:T(8,128)} %fusion.162, bf16[3,64,4096]{2,1,0:T(8,128)(2,1)} %get-tuple-element.601, s32[]{:T(128)S(6)} %select_n.97), kind=kOutput, calls=%fused_computation.34.clone.1 | convolution fusion | flops 313789440 | bytes 38732292 | tf_op jit(solution)/shard_map/while/body/eval_jaxpr/hqk,hdk->hdq/dot_general | solution.py:100
  502.4 6.1 fusion.164
  512.5 7.5 subtract_exponential_fusion.4
  520.0 6.2 fusion.162
  526.3 15.8 %fusion.163 = f32[3,64,4096]{2,1,0:T(8,128)} fusion(f32[3,64,4096]{2,1,0:T(8,128)} %get-tuple-element.577, s32[]{:T(128)S(6)} %select_n.97, f32[3,512,1536]{2,1,0:T(8,128)} %subtract_exponential_fusion.4, f32[3,512,1536]{2,1,0:T(8,128)} %fusion.162, bf16[3,64,3072]{2,1,0:T(8,128)(2,1)} %get-tuple-element.598, s32[]{:T(128)S(6)} %select_n.98), kind=kOutput, calls=%fused_computation.31.clone.1 | convolution fusion | flops 314084352 | bytes 40304648 | tf_op jit(solution)/shard_map/while/body/eval_jaxpr/hqk,hdq->hdk/dot_general | solution.py:103
  542.1 15.4 %fusion.165 = bf16[6,3,64,512]{3,2,1,0:T(8,128)(2,1)} fusion(bf16[6,3,64,512]{3,2,1,0:T(8,128)(2,1)} %get-tuple-element.579, s32[]{:T(128)} %get-tuple-element.576, f32[3,512,1536]{2,1,0:T(8,128)} %subtract_exponential_fusion.4, f32[3,512,1536]{2,1,0:T(8,128)} %fusion.162, bf16[3,64,4096]{2,1,0:T(8,128)(2,1)} %get-tuple-element.601, s32[]{:T(128)S(6)} %select_n.97), kind=kOutput, calls=%fused_computation.34.clone.1 | convolution fusion | flops 313789440 | bytes 38732292 | tf_op jit(solution)/shard_map/while/body/eval_jaxpr/hqk,hdk->hdq/dot_general | solution.py:100
  557.5 6.1 fusion.164
  567.5 7.3 subtract_exponential_fusion.4
  574.9 6.3 fusion.162
  581.2 17.1 %fusion.163 = f32[3,64,4096]{2,1,0:T(8,128)} fusion(f32[3,64,4096]{2,1,0:T(8,128)} %get-tuple-element.577, s32[]{:T(128)S(6)} %select_n.97, f32[3,512,1536]{2,1,0:T(8,128)} %subtract_exponential_fusion.4, f32[3,512,1536]{2,1,0:T(8,128)} %fusion.162, bf16[3,64,3072]{2,1,0:T(8,128)(2,1)} %get-tuple-element.598, s32[]{:T(128)S(6)} %select_n.98), kind=kOutput, calls=%fused_computation.31.clone.1 | convolution fusion | flops 314084352 | bytes 40304648 | tf_op jit(solution)/shard_map/while/body/eval_jaxpr/hqk,hdq->hdk/dot_general | solution.py:103
  598.3 16.7 %fusion.165 = bf16[6,3,64,512]{3,2,1,0:T(8,128)(2,1)} fusion(bf16[6,3,64,512]{3,2,1,0:T(8,128)(2,1)} %get-tuple-element.579, s32[]{:T(128)} %get-tuple-element.576, f32[3,512,1536]{2,1,0:T(8,128)} %subtract_exponential_fusion.4, f32[3,512,1536]{2,1,0:T(8,128)} %fusion.162, bf16[3,64,4096]{2,1,0:T(8,128)(2,1)} %get-tuple-element.601, s32[]{:T(128)S(6)} %select_n.97), kind=kOutput, calls=%fused_computation.34.clone.1 | convolution fusion | flops 313789440 | bytes 38732292 | tf_op jit(solution)/shard_map/while/body/eval_jaxpr/hqk,hdk->hdq/dot_general | solution.py:100
  615.0 6.1 fusion.164
  625.1 7.3 subtract_exponential_fusion.4
  632.4 6.2 fusion.162
  638.7 16.1 %fusion.163 = f32[3,64,4096]{2,1,0:T(8,128)} fusion(f32[3,64,4096]{2,1,0:T(8,128)} %get-tuple-element.577, s32[]{:T(128)S(6)} %select_n.97, f32[3,512,1536]{2,1,0:T(8,128)} %subtract_exponential_fusion.4, f32[3,512,1536]{2,1,0:T(8,128)} %fusion.162, bf16[3,64,3072]{2,1,0:T(8,128)(2,1)} %get-tuple-element.598, s32[]{:T(128)S(6)} %select_n.98), kind=kOutput, calls=%fused_computation.31.clone.1 | convolution fusion | flops 314084352 | bytes 40304648 | tf_op jit(solution)/shard_map/while/body/eval_jaxpr/hqk,hdq->hdk/dot_general | solution.py:103
  654.8 15.4 %fusion.165 = bf16[6,3,64,512]{3,2,1,0:T(8,128)(2,1)} fusion(bf16[6,3,64,512]{3,2,1,0:T(8,128)(2,1)} %get-tuple-element.579, s32[]{:T(128)} %get-tuple-element.576, f32[3,512,1536]{2,1,0:T(8,128)} %subtract_exponential_fusion.4, f32[3,512,1536]{2,1,0:T(8,128)} %fusion.162, bf16[3,64,4096]{2,1,0:T(8,128)(2,1)} %get-tuple-element.601, s32[]{:T(128)S(6)} %select_n.97), kind=kOutput, calls=%fused_computation.34.clone.1 | convolution fusion | flops 313789440 | bytes 38732292 | tf_op jit(solution)/shard_map/while/body/eval_jaxpr/hqk,hdk->hdq/dot_general | solution.py:100
  670.2 6.1 fusion.164
  680.3 7.3 subtract_exponential_fusion.4
  687.7 6.2 fusion.162
  693.9 15.8 %fusion.163 = f32[3,64,4096]{2,1,0:T(8,128)} fusion(f32[3,64,4096]{2,1,0:T(8,128)} %get-tuple-element.577, s32[]{:T(128)S(6)} %select_n.97, f32[3,512,1536]{2,1,0:T(8,128)} %subtract_exponential_fusion.4, f32[3,512,1536]{2,1,0:T(8,128)} %fusion.162, bf16[3,64,3072]{2,1,0:T(8,128)(2,1)} %get-tuple-element.598, s32[]{:T(128)S(6)} %select_n.98), kind=kOutput, calls=%fused_computation.31.clone.1 | convolution fusion | flops 314084352 | bytes 40304648 | tf_op jit(solution)/shard_map/while/body/eval_jaxpr/hqk,hdq->hdk/dot_general | solution.py:103
  709.7 15.7 %fusion.165 = bf16[6,3,64,512]{3,2,1,0:T(8,128)(2,1)} fusion(bf16[6,3,64,512]{3,2,1,0:T(8,128)(2,1)} %get-tuple-element.579, s32[]{:T(128)} %get-tuple-element.576, f32[3,512,1536]{2,1,0:T(8,128)} %subtract_exponential_fusion.4, f32[3,512,1536]{2,1,0:T(8,128)} %fusion.162, bf16[3,64,4096]{2,1,0:T(8,128)(2,1)} %get-tuple-element.601, s32[]{:T(128)S(6)} %select_n.97), kind=kOutput, calls=%fused_computation.34.clone.1 | convolution fusion | flops 313789440 | bytes 38732292 | tf_op jit(solution)/shard_map/while/body/eval_jaxpr/hqk,hdk->hdq/dot_general | solution.py:100
  725.4 6.5 fusion.164
  735.9 7.4 subtract_exponential_fusion.4
  743.3 6.3 fusion.162
  749.6 15.9 %fusion.163 = f32[3,64,4096]{2,1,0:T(8,128)} fusion(f32[3,64,4096]{2,1,0:T(8,128)} %get-tuple-element.577, s32[]{:T(128)S(6)} %select_n.97, f32[3,512,1536]{2,1,0:T(8,128)} %subtract_exponential_fusion.4, f32[3,512,1536]{2,1,0:T(8,128)} %fusion.162, bf16[3,64,3072]{2,1,0:T(8,128)(2,1)} %get-tuple-element.598, s32[]{:T(128)S(6)} %select_n.98), kind=kOutput, calls=%fused_computation.31.clone.1 | convolution fusion | flops 314084352 | bytes 40304648 | tf_op jit(solution)/shard_map/while/body/eval_jaxpr/hqk,hdq->hdk/dot_general | solution.py:103
  765.4 15.4 %fusion.165 = bf16[6,3,64,512]{3,2,1,0:T(8,128)(2,1)} fusion(bf16[6,3,64,512]{3,2,1,0:T(8,128)(2,1)} %get-tuple-element.579, s32[]{:T(128)} %get-tuple-element.576, f32[3,512,1536]{2,1,0:T(8,128)} %subtract_exponential_fusion.4, f32[3,512,1536]{2,1,0:T(8,128)} %fusion.162, bf16[3,64,4096]{2,1,0:T(8,128)(2,1)} %get-tuple-element.601, s32[]{:T(128)S(6)} %select_n.97), kind=kOutput, calls=%fused_computation.34.clone.1 | convolution fusion | flops 313789440 | bytes 38732292 | tf_op jit(solution)/shard_map/while/body/eval_jaxpr/hqk,hdk->hdq/dot_general | solution.py:100
  780.8 6.1 fusion.164
  799.9 10.0 copy.165
  809.9 157.8 %all_to_all.62 = bf16[3,192,3072]{1,0,2:T(4,128)(2,1)} all-to-all(bf16[3,192,3072]{1,0,2:T(4,128)(2,1)} %copy.165), channel_id=1, replica_groups=mesh['seq'=8,'head'=4] {'head'}, dimensions={2} | all-to-all | bytes 7077888 | tf_op jit(solution)/shard_map/all_to_all | solution.py:275
  967.7 9.8 copy.167
  977.5 8.1 convolution_bitcast_fusion
  985.7 8.0 copy.179
  997.9 10.8 copy.177
  1017.9 41.1 %all-reduce.14 = (f32[768]{0:T(1024)}, f32[768]{0:T(1024)}, f32[768]{0:T(1024)}, f32[768]{0:T(1024)}, f32[768]{0:T(1024)}, /*index=5*/f32[3072]{0:T(1024)}, f32[...) all-reduce(f32[768]{0:T(1024)} %reduce_sum.241, ...), channel_id=3, replica_groups=mesh['seq'=8,'head'=4] {'seq','head'}, use_global_device_ids=true, to_apply=%region_22.23.clone | all-reduce | flops 12289 | bytes 98312
  1070.3 6.5 convolution_add_fusion
  1083.2 29.1 %reduce-scatter.17.cloned.1.call-done = f32[24,2304]{1,0:T(8,128)} async-done(((f32[768,2304]{1,0:T(8,128)}), f32[24,2304]{1,0:T(8,128)}) %reduce-scatter.17.cloned.1.call-update) | async-done | bytes 221200
  (298 shorter events, 209.0 us)
Async XLA Ops:
  7.2 2.0 copy-start
  19.5 6.7 copy-start.37
  19.5 111.4 %all-to-all-start = ((bf16[3,768,768]{2,0,1:T(4,128)(2,1)}), bf16[3,768,768]{2,0,1:T(4,128)(2,1)}, u32[]{:S(2)}, u32[]{:S(2)}) async-start(bf16[3,768,768]{2,0,1:T(4,128)(2,1)} %copy.152), calls=%async_computation | async-start | bytes 9437184 | tf_op jit(solution)/shard_map/all_to_all | solution.py:179
  155.4 5.4 copy-start.4
  168.0 1.3 copy-start.44
  177.9 4.8 copy-start.45
  182.8 1.2 copy-start.44
  192.7 4.8 copy-start.45
  197.5 1.2 copy-start.44
  207.5 4.8 copy-start.45
  212.3 1.2 copy-start.44
  222.3 4.8 copy-start.45
  237.1 4.8 copy-start.45
  251.9 4.8 copy-start.45
  266.0 32.5 %copy-start.40 = (f32[768]{0:T(1024)S(1)}, f32[768]{0:T(1024)}, u32[]{:S(2)}) copy-start(f32[768]{0:T(1024)} %param.32) | copy-start | bytes 9220
  266.0 32.5 %all-to-all-start.1 = ((bf16[192,4,768]{2,0,1:T(8,128)(2,1)}), bf16[192,4,768]{2,0,1:T(8,128)(2,1)}, u32[]{:S(2)}, u32[]{:S(2)}) async-start(bf16[192,4,768]{2,0,1:T(8,128)(2,1)} %copy.158), calls=%async_computation.1 | async-start | bytes 2359296 | tf_op jit(solution)/shard_map/all_to_all | solution.py:184
  270.4 812.8 %reduce-scatter.15.cloned.1.call-start = ((), (), s32[]{:S(2)}) async-start(), calls=%async_computation.12 | async-start | bytes 2433024 | tf_op jit(solution)/shard_map/reduce_scatter | solution.py:300
  275.2 18.6 %copy-start.19 = (s32[768]{0:T(1024)}, s32[768]{0:T(1024)S(1)}, u32[]{:S(2)}) copy-start(s32[768]{0:T(1024)S(1)} %iota_add_fusion) | copy-start | bytes 9220
  298.4 3.7 copy-start.33
  298.4 3.8 copy-start.38
  298.4 3.8 copy-start.42
  298.5 34.1 %slice-start = ((s8[4718592]{0:T(1024)(128)(4,1)}), s8[4194304]{0:T(1024)(128)(4,1)S(1)}, s32[]{:S(2)}) async-start(s8[4718592]{0:T(1024)(128)(4,1)} %bitcast.131), calls=%async_computation.14 | async-start | bytes 8388608
  301.9 30.7 %copy-start.5 = (f32[768,768]{0,1:T(8,128)}, f32[768,768]{0,1:T(8,128)S(1)}, u32[]{:S(2)}) copy-start(f32[768,768]{0,1:T(8,128)S(1)} %get-tuple-element.372) | copy-start | bytes 7077892
  301.9 30.7 %copy-start.17 = (f32[768]{0:T(1024)}, f32[768]{0:T(1024)S(1)}, u32[]{:S(2)}) copy-start(f32[768]{0:T(1024)S(1)} %broadcast_multiply_fusion.5) | copy-start | bytes 9220
  302.2 30.3 %copy-start.24 = (f32[768]{0:T(1024)}, f32[768]{0:T(1024)S(1)}, u32[]{:S(2)}) copy-start(f32[768]{0:T(1024)S(1)} %add_rsqrt_fusion.1) | copy-start | bytes 9220
  302.2 30.3 %slice-start.1 = ((s8[4718592]{0:T(1024)(128)(4,1)}), s8[524288]{0:T(1024)(128)(4,1)S(1)}, s32[]{:S(2)}) async-start(s8[4718592]{0:T(1024)(128)(4,1)} %bitcast.131), calls=%async_computation.15 | async-start | bytes 1048576
  302.2 30.3 %copy-start.41 = (f32[768]{0:T(1024)S(1)}, f32[768]{0:T(1024)}, u32[]{:S(2)}) copy-start(f32[768]{0:T(1024)} %param.38) | copy-start | bytes 9220
  332.5 4.9 copy-start.46
  332.6 5.2 copy-start.16
  332.6 5.2 copy-start.31
  337.4 1.5 copy-start.1
  337.5 2.2 copy-start.8
  337.5 2.2 copy-start.32
  337.8 2.2 copy-start.15
  337.8 2.8 copy-start.29
  337.8 2.8 copy-start.36
  338.2 1.7 copy-start.3
  339.6 4.8 copy-start.26
  340.2 1.3 copy-start.13
  340.2 1.3 copy-start.21
  340.2 1.3 copy-start.27
  349.5 3.2 copy-start.35
  352.6 730.6 %reduce-scatter.9.cloned.1.call-start = ((), (), s32[]{:S(2)}) async-start(), calls=%async_computation.9 | async-start | bytes 2433024 | tf_op jit(solution)/shard_map/reduce_scatter | solution.py:290
  352.6 4.6 copy-start.2
  357.3 1.5 copy-start.39
  357.3 16.9 %slice-start.2 = ((s8[4718592]{0:T(1024)(128)(4,1)}), s8[4194304]{0:T(1024)(128)(4,1)S(1)}, s32[]{:S(2)}) async-start(s8[4718592]{0:T(1024)(128)(4,1)} %bitcast.133), calls=%async_computation.16 | async-start | bytes 8388608
  358.8 15.5 %copy-start.10 = (f32[768,768]{0,1:T(8,128)}, f32[768,768]{0,1:T(8,128)S(1)}, u32[]{:S(2)}) copy-start(f32[768,768]{0,1:T(8,128)S(1)} %get-tuple-element.334) | copy-start | bytes 7077892
  358.8 15.5 %copy-start.6 = (f32[768,768]{0,1:T(8,128)S(1)}, f32[768,768]{0,1:T(8,128)}, u32[]{:S(2)}) copy-start(f32[768,768]{0,1:T(8,128)} %copy-done.5) | copy-start | bytes 7077892
  358.8 15.5 %copy-start.18 = (f32[768]{0:T(1024)S(1)}, f32[768]{0:T(1024)}, u32[]{:S(2)}) copy-start(f32[768]{0:T(1024)} %copy-done.17) | copy-start | bytes 9220
  358.8 15.5 %copy-start.25 = (f32[768]{0:T(1024)S(1)}, f32[768]{0:T(1024)}, u32[]{:S(2)}) copy-start(f32[768]{0:T(1024)} %copy-done.24) | copy-start | bytes 9220
  358.8 15.5 %copy-start.34 = (f32[768]{0:T(1024)S(1)}, f32[768]{0:T(1024)}, u32[]{:S(2)}) copy-start(f32[768]{0:T(1024)} %param.33) | copy-start | bytes 9220
  358.8 15.5 %slice-start.3 = ((s8[4718592]{0:T(1024)(128)(4,1)}), s8[524288]{0:T(1024)(128)(4,1)S(1)}, s32[]{:S(2)}) async-start(s8[4718592]{0:T(1024)(128)(4,1)} %bitcast.133), calls=%async_computation.17 | async-start | bytes 1048576
  383.2 1.4 copy-start.7
  384.7 4.3 copy-start.43
  388.6 694.6 %reduce-scatter.11.cloned.1.call-start = ((), (), s32[]{:S(2)}) async-start(), calls=%async_computation.10 | async-start | bytes 9732096 | tf_op jit(solution)/shard_map/reduce_scatter | solution.py:294
  403.9 37.8 %all-to-all-start.2 = ((bf16[4,192,768]{2,1,0:T(8,128)(2,1)}), bf16[4,192,768]{2,1,0:T(8,128)(2,1)}, u32[]{:S(2)}, u32[]{:S(2)}) async-start(bf16[4,192,768]{2,1,0:T(8,128)(2,1)} %bitcast.127), calls=%async_computation.2 | async-start | bytes 2359296 | tf_op jit(solution)/shard_map/all_to_all | solution.py:262
  408.2 675.0 %reduce-scatter.13.cloned.1.call-start = ((), (), s32[]{:S(2)}) async-start(), calls=%async_computation.11 | async-start | bytes 9732096 | tf_op jit(solution)/shard_map/reduce_scatter | solution.py:296
  419.0 693.2 %reduce-scatter.17.cloned.1.call-start = ((), (), s32[]{:S(2)}) async-start(), calls=%async_computation.13 | async-start | bytes 7299072
  794.1 3.8 copy-start.9
  993.7 2.4 copy-start.14
  993.7 2.4 copy-start.22
  993.7 2.4 copy-start.28
  993.7 2.5 copy-start.30
  997.9 20.0 %copy-start.23 = (f32[768]{0:T(1024)S(1)}, f32[768]{0:T(1024)}, u32[]{:S(2)}) copy-start(f32[768]{0:T(1024)} %get-tuple-element.269) | copy-start | bytes 9220
  (5 other events, 4.5 us)
Sparse Core Ops, SparseCore 0:
  352.7 107.4 reduce-scatter.14
  466.0 98.6 reduce-scatter.8
  571.2 135.1 reduce-scatter.10
  712.7 149.2 reduce-scatter.12
  993.8 118.3 reduce-scatter.16
where the time goes:
time: 1130 us; the launch traced here: 1120 us
  matrix products  474 us (42%)
  blocking collectives  199 us (18%)
  local copies, waits for them, and re-layouts  187 us (17%)
  waiting for transfers between devices  157 us (14%)
  other arithmetic  62.6 us (6%)
  between operations  16.5 us (1%)
  starting transfers between devices  15.9 us (1%)
    all_to_all x1, blocking collectives, local(): lax.all_to_all(grad_stack, 'head', split_axis=2, concat_axis=1, tiled=True)  158 us
    all_to_all x1, waiting for transfers between devices, local(): lax.all_to_all(qkv_low, 'head', split_axis=1, concat_axis=2, tiled=True)  102 us
    dot_general x6, matrix products, one_block(): jnp.einsum('hqk,hdq->hdk', grad_scores, q_block, preferred_element_type=j...  96.5 us
    dot_general x6, matrix products, one_block(): jnp.einsum('hqk,hdk->hdq', grad_scores, k_window, preferred_element_type=...  94.1 us
    dot_general x12, matrix products, block_scores(): jnp.einsum('hdq,hdk->hqk', q_block, k_window, preferred_element_type=jnp....  63.4 us
    unnamed x1, blocking collectives  41.1 us
    dot_general x6, matrix products, one_block(): jnp.einsum('hdq,hdk->hqk', grad_block, v_window, preferred_element_type=j...  37.6 us
    dot_general x6, matrix products, one_block(): jnp.einsum('hqk,hdq->hdk', weights_low, grad_block, preferred_element_typ...  37 us
  transfers between devices with their start and end apart: 8, of which 4 were waited for; matrix products, arithmetic and copies ran while one was open for 47% of the time, Pallas kernels for 0%

commit v1 on v0

--- a/solution.py
+++ b/solution.py
@@ -157,6 +157,14 @@
     b_pool,
     w_class,
 ):
+
+    def tiles_divide(mine_x, across):
+        big = jnp.split(mine_x, lax.psum(1, axis_name=across), axis=0)
+        ready = lax.all_to_all(
+            jnp.stack(big, axis=0), axis_name=across, split_axis=0, concat_axis=0
+        )
+        return jnp.concatenate(ready, axis=1)
+
     n_head = lax.axis_size("head")
     n_seq = lax.axis_size("seq")
     head_index = lax.axis_index("head")
@@ -259,9 +267,7 @@
     grad_ctx_cols = lax.dot_general(
         w_out, grad_attn, contract_last, preferred_element_type=jnp.float32
     )
-    grad_ctx_heads = lax.all_to_all(
-        grad_ctx_cols.astype(jnp.bfloat16), "head", split_axis=0, concat_axis=1, tiled=True
-    )
+    grad_ctx_heads = tiles_divide(grad_ctx_cols.astype(jnp.bfloat16), "head")
     grad_q, grad_k, grad_v = attend_backward(
         q_heads,
         k_heads,

time: 1130 us -> 1130 us (level)
    unnamed x114 -> x118, local copies, waits for them, and re-layouts: 36.9 us -> 39.3 us
where the time goes in v1:
time: 1130 us; the launch traced here: 1120 us
  matrix products  471 us (42%)
  blocking collectives  199 us (18%)
  local copies, waits for them, and re-layouts  190 us (17%)
  waiting for transfers between devices  156 us (14%)
  other arithmetic  63.8 us (6%)
  between operations  16.4 us (1%)
  starting transfers between devices  15.8 us (1%)
    all_to_all x1, blocking collectives, local(): lax.all_to_all(grad_stack, 'head', split_axis=2, concat_axis=1, tiled=True)  158 us
    all_to_all x1, waiting for transfers between devices, local(): lax.all_to_all(qkv_low, 'head', split_axis=1, concat_axis=2, tiled=True)  102 us
    dot_general x6, matrix products, one_block(): jnp.einsum('hqk,hdq->hdk', grad_scores, q_block, preferred_element_type=j...  96.5 us
    dot_general x6, matrix products, one_block(): jnp.einsum('hqk,hdk->hdq', grad_scores, k_window, preferred_element_type=...  94.1 us
    dot_general x12, matrix products, block_scores(): jnp.einsum('hdq,hdk->hqk', q_block, k_window, preferred_element_type=jnp....  63.4 us
    unnamed x1, blocking collectives  41.1 us
    unnamed x118, local copies, waits for them, and re-layouts  39.3 us
    dot_general x6, matrix products, one_block(): jnp.einsum('hdq,hdk->hqk', grad_block, v_window, preferred_element_type=j...  37.6 us
  transfers between devices with their start and end apart: 8, of which 4 were waited for; matrix products, arithmetic and copies ran while one was open for 47% of the time, Pallas kernels for 0%

profile of v1, /device:TPU:0, one launch (start us, length us, event | category | flops | bytes accessed | tf_op | source)
XLA Modules:
  0.0 1120.0 jit_solution(7994036309650244012)
XLA Ops:
  9.2 5.1 add_convert_fusion.1
  14.3 5.2 copy.151
  19.5 6.7 all-to-all-start
  29.1 101.8 %all-to-all-done = bf16[3,768,768]{2,0,1:T(4,128)(2,1)} async-done(((bf16[3,768,768]{2,0,1:T(4,128)(2,1)}), bf16[3,768,768]{2,0,1:T(4,128)(2,1)}, u32[]{:S(2)}, u32[]{:S(2)}) %all-to-all-start) | async-done | bytes 3538976 | tf_op jit(solution)/shard_map/all_to_all | solution.py:187
  130.9 11.1 fusion.93
  167.8 88.9 %while.26 = (s32[]{:T(128)}, bf16[6,3,64,512]{3,2,1,0:T(8,128)(2,1)}, f32[6,3,512]{2,1,0:T(4,128)}, s32[6]{0:T(128)S(1)}, bf16[3,64,4096]{2,1,0:T(8,128)(2,1)}, ...) while((s32[]{:T(128)}, ...), condition=%wide.region_5.6_spmd, body=%wide.region_2.5_spmd.sunk | while | flops 633076224 | bytes 33304036 | solution.py:69
  177.9 4.8 fusion.152
  192.7 4.8 fusion.152
  207.5 4.8 fusion.152
  222.3 4.8 fusion.152
  237.1 4.8 fusion.152
  251.9 4.8 fusion.152
  266.0 4.3 all-to-all-start.1
  276.4 16.7 %fusion.72 = (pred[768]{0:T(1024)(128)(4,1)}, s32[768]{0:T(1024)S(1)}) fusion(s32[]{:T(128)} %bitcast.16, s32[]{:T(128)} %bitcast.17, s32[]{:T(128)} %bitcast.18, s32[]{:T(128)} %bitcast.19, s32[]{:T(128)} %bitcast.20, s32[]{:T(128)} %bitcast.21, s32[]{:T(128)} %bitcast.22, s32[]{:T(128)} %bitcast.23, s32[]{:T(128)} %bitcast.24, s32[]{:T(128)} %bitcast.25, ...), kind=kLoop, calls=%fused_computation.126 | loop fusion | flops 42240 | bytes 7016 | tf_op jit(solution)/shard_map/eq | solution.py:214
  303.5 28.5 %multiply_convert_fusion.1 = (bf16[768,3072]{1,0:T(8,128)(2,1)S(1)}, f32[768,3072]{1,0:T(8,128)}, f32[768,3072]{1,0:T(8,128)}) fusion(f32[3072]{0:T(1024)S(1)} %copy-done.38, bf16[768,3072]{1,0:T(8,128)(2,1)S(1)} %bitcast.140, f32[768,768]{0,1:T(8,128)S(1)} %get-tuple-element.376, f32[768]{0:T(1024)S(1)} %copy-done.42, f32[768]{0:T(1024)S(1)} %copy-done.33, ...), kind=kOutput, calls=%fused_computation.57 | convolution fusion | flops 3782541312 | bytes 30695424 | tf_op jit(solution)/shard_map/dot_general | solution.py:203
  332.1 4.6 fusion.97
  344.0 5.0 gather_fusion
  352.7 4.6 multiply_reduce_fusion.1
  358.9 15.4 %convert_reduce_fusion = (f32[3072]{0:T(1024)}, bf16[768,3072]{1,0:T(8,128)(2,1)}) fusion(f32[768,3072]{1,0:T(8,128)} %get-tuple-element.341, bf16[3072,768]{1,0:T(8,128)(2,1)} %param.37, f32[768,768]{0,1:T(8,128)S(1)} %get-tuple-element.334, f32[768,3072]{1,0:T(8,128)} %get-tuple-element.377, f32[3072]{0:T(1024)S(1)} %copy-done.39), kind=kOutput, calls=%fused_computation.55 | convolution fusion | flops 3664573440 | bytes 30695424 | tf_op jit(solution)/shard_map/dot_general | solution.py:252
  374.3 7.5 multiply_reduce_fusion.2
  389.3 10.6 fusion.99
  404.3 4.3 all-to-all-start.2
  408.7 10.8 fusion.84
  419.6 21.9 %all-to-all-done.2 = bf16[4,192,768]{2,1,0:T(8,128)(2,1)} async-done(((bf16[4,192,768]{2,1,0:T(8,128)(2,1)}), bf16[4,192,768]{2,1,0:T(8,128)(2,1)}, u32[]{:S(2)}, u32[]{:S(2)}) %all-to-all-start.2) | async-done | bytes 1179680 | tf_op jit(solution)/shard_map/all_to_all | solution.py:163
  453.3 333.5 %while.27 = (s32[]{:T(128)}, f32[3,64,4096]{2,1,0:T(8,128)}, f32[3,64,4096]{2,1,0:T(8,128)}, bf16[6,3,64,512]{3,2,1,0:T(8,128)(2,1)}, s32[6]{0:T(128)S(1)}, /*in...) while((s32[]{:T(128)}, f32[3,64,4096]{2,1,0:T(8,128)}, ...), condition=%wide.region_19.20_spmd, body=%wide.region_17.19_spmd.sunk | while | flops 1544361984 | bytes 113093408 | solution.py:125
  457.3 7.3 subtract_exponential_fusion.4
  464.7 6.2 fusion.163
  470.9 15.8 %fusion.164 = f32[3,64,4096]{2,1,0:T(8,128)} fusion(f32[3,64,4096]{2,1,0:T(8,128)} %get-tuple-element.581, s32[]{:T(128)S(6)} %select_n.97, f32[3,512,1536]{2,1,0:T(8,128)} %subtract_exponential_fusion.4, f32[3,512,1536]{2,1,0:T(8,128)} %fusion.163, bf16[3,64,3072]{2,1,0:T(8,128)(2,1)} %get-tuple-element.602, s32[]{:T(128)S(6)} %select_n.98), kind=kOutput, calls=%fused_computation.31.clone.1 | convolution fusion | flops 314084352 | bytes 40304648 | tf_op jit(solution)/shard_map/while/body/eval_jaxpr/hqk,hdq->hdk/dot_general | solution.py:103
  486.8 15.5 %fusion.166 = bf16[6,3,64,512]{3,2,1,0:T(8,128)(2,1)} fusion(bf16[6,3,64,512]{3,2,1,0:T(8,128)(2,1)} %get-tuple-element.583, s32[]{:T(128)} %get-tuple-element.580, f32[3,512,1536]{2,1,0:T(8,128)} %subtract_exponential_fusion.4, f32[3,512,1536]{2,1,0:T(8,128)} %fusion.163, bf16[3,64,4096]{2,1,0:T(8,128)(2,1)} %get-tuple-element.605, s32[]{:T(128)S(6)} %select_n.97), kind=kOutput, calls=%fused_computation.34.clone.1 | convolution fusion | flops 313789440 | bytes 38732292 | tf_op jit(solution)/shard_map/while/body/eval_jaxpr/hqk,hdk->hdq/dot_general | solution.py:100
  502.2 6.1 fusion.165
  512.3 7.5 subtract_exponential_fusion.4
  519.9 6.2 fusion.163
  526.1 15.8 %fusion.164 = f32[3,64,4096]{2,1,0:T(8,128)} fusion(f32[3,64,4096]{2,1,0:T(8,128)} %get-tuple-element.581, s32[]{:T(128)S(6)} %select_n.97, f32[3,512,1536]{2,1,0:T(8,128)} %subtract_exponential_fusion.4, f32[3,512,1536]{2,1,0:T(8,128)} %fusion.163, bf16[3,64,3072]{2,1,0:T(8,128)(2,1)} %get-tuple-element.602, s32[]{:T(128)S(6)} %select_n.98), kind=kOutput, calls=%fused_computation.31.clone.1 | convolution fusion | flops 314084352 | bytes 40304648 | tf_op jit(solution)/shard_map/while/body/eval_jaxpr/hqk,hdq->hdk/dot_general | solution.py:103
  541.9 15.4 %fusion.166 = bf16[6,3,64,512]{3,2,1,0:T(8,128)(2,1)} fusion(bf16[6,3,64,512]{3,2,1,0:T(8,128)(2,1)} %get-tuple-element.583, s32[]{:T(128)} %get-tuple-element.580, f32[3,512,1536]{2,1,0:T(8,128)} %subtract_exponential_fusion.4, f32[3,512,1536]{2,1,0:T(8,128)} %fusion.163, bf16[3,64,4096]{2,1,0:T(8,128)(2,1)} %get-tuple-element.605, s32[]{:T(128)S(6)} %select_n.97), kind=kOutput, calls=%fused_computation.34.clone.1 | convolution fusion | flops 313789440 | bytes 38732292 | tf_op jit(solution)/shard_map/while/body/eval_jaxpr/hqk,hdk->hdq/dot_general | solution.py:100
  557.3 6.1 fusion.165
  567.3 7.3 subtract_exponential_fusion.4
  574.7 6.3 fusion.163
  581.0 17.1 %fusion.164 = f32[3,64,4096]{2,1,0:T(8,128)} fusion(f32[3,64,4096]{2,1,0:T(8,128)} %get-tuple-element.581, s32[]{:T(128)S(6)} %select_n.97, f32[3,512,1536]{2,1,0:T(8,128)} %subtract_exponential_fusion.4, f32[3,512,1536]{2,1,0:T(8,128)} %fusion.163, bf16[3,64,3072]{2,1,0:T(8,128)(2,1)} %get-tuple-element.602, s32[]{:T(128)S(6)} %select_n.98), kind=kOutput, calls=%fused_computation.31.clone.1 | convolution fusion | flops 314084352 | bytes 40304648 | tf_op jit(solution)/shard_map/while/body/eval_jaxpr/hqk,hdq->hdk/dot_general | solution.py:103
  598.1 16.7 %fusion.166 = bf16[6,3,64,512]{3,2,1,0:T(8,128)(2,1)} fusion(bf16[6,3,64,512]{3,2,1,0:T(8,128)(2,1)} %get-tuple-element.583, s32[]{:T(128)} %get-tuple-element.580, f32[3,512,1536]{2,1,0:T(8,128)} %subtract_exponential_fusion.4, f32[3,512,1536]{2,1,0:T(8,128)} %fusion.163, bf16[3,64,4096]{2,1,0:T(8,128)(2,1)} %get-tuple-element.605, s32[]{:T(128)S(6)} %select_n.97), kind=kOutput, calls=%fused_computation.34.clone.1 | convolution fusion | flops 313789440 | bytes 38732292 | tf_op jit(solution)/shard_map/while/body/eval_jaxpr/hqk,hdk->hdq/dot_general | solution.py:100
  614.8 6.1 fusion.165
  625.0 7.3 subtract_exponential_fusion.4
  632.3 6.2 fusion.163
  638.5 16.1 %fusion.164 = f32[3,64,4096]{2,1,0:T(8,128)} fusion(f32[3,64,4096]{2,1,0:T(8,128)} %get-tuple-element.581, s32[]{:T(128)S(6)} %select_n.97, f32[3,512,1536]{2,1,0:T(8,128)} %subtract_exponential_fusion.4, f32[3,512,1536]{2,1,0:T(8,128)} %fusion.163, bf16[3,64,3072]{2,1,0:T(8,128)(2,1)} %get-tuple-element.602, s32[]{:T(128)S(6)} %select_n.98), kind=kOutput, calls=%fused_computation.31.clone.1 | convolution fusion | flops 314084352 | bytes 40304648 | tf_op jit(solution)/shard_map/while/body/eval_jaxpr/hqk,hdq->hdk/dot_general | solution.py:103
  654.7 15.4 %fusion.166 = bf16[6,3,64,512]{3,2,1,0:T(8,128)(2,1)} fusion(bf16[6,3,64,512]{3,2,1,0:T(8,128)(2,1)} %get-tuple-element.583, s32[]{:T(128)} %get-tuple-element.580, f32[3,512,1536]{2,1,0:T(8,128)} %subtract_exponential_fusion.4, f32[3,512,1536]{2,1,0:T(8,128)} %fusion.163, bf16[3,64,4096]{2,1,0:T(8,128)(2,1)} %get-tuple-element.605, s32[]{:T(128)S(6)} %select_n.97), kind=kOutput, calls=%fused_computation.34.clone.1 | convolution fusion | flops 313789440 | bytes 38732292 | tf_op jit(solution)/shard_map/while/body/eval_jaxpr/hqk,hdk->hdq/dot_general | solution.py:100
  670.1 6.1 fusion.165
  680.2 7.3 subtract_exponential_fusion.4
  687.5 6.2 fusion.163
  693.7 15.8 %fusion.164 = f32[3,64,4096]{2,1,0:T(8,128)} fusion(f32[3,64,4096]{2,1,0:T(8,128)} %get-tuple-element.581, s32[]{:T(128)S(6)} %select_n.97, f32[3,512,1536]{2,1,0:T(8,128)} %subtract_exponential_fusion.4, f32[3,512,1536]{2,1,0:T(8,128)} %fusion.163, bf16[3,64,3072]{2,1,0:T(8,128)(2,1)} %get-tuple-element.602, s32[]{:T(128)S(6)} %select_n.98), kind=kOutput, calls=%fused_computation.31.clone.1 | convolution fusion | flops 314084352 | bytes 40304648 | tf_op jit(solution)/shard_map/while/body/eval_jaxpr/hqk,hdq->hdk/dot_general | solution.py:103
  709.5 15.7 %fusion.166 = bf16[6,3,64,512]{3,2,1,0:T(8,128)(2,1)} fusion(bf16[6,3,64,512]{3,2,1,0:T(8,128)(2,1)} %get-tuple-element.583, s32[]{:T(128)} %get-tuple-element.580, f32[3,512,1536]{2,1,0:T(8,128)} %subtract_exponential_fusion.4, f32[3,512,1536]{2,1,0:T(8,128)} %fusion.163, bf16[3,64,4096]{2,1,0:T(8,128)(2,1)} %get-tuple-element.605, s32[]{:T(128)S(6)} %select_n.97), kind=kOutput, calls=%fused_computation.34.clone.1 | convolution fusion | flops 313789440 | bytes 38732292 | tf_op jit(solution)/shard_map/while/body/eval_jaxpr/hqk,hdk->hdq/dot_general | solution.py:100
  725.3 6.5 fusion.165
  735.8 7.4 subtract_exponential_fusion.4
  743.1 6.3 fusion.163
  749.4 15.8 %fusion.164 = f32[3,64,4096]{2,1,0:T(8,128)} fusion(f32[3,64,4096]{2,1,0:T(8,128)} %get-tuple-element.581, s32[]{:T(128)S(6)} %select_n.97, f32[3,512,1536]{2,1,0:T(8,128)} %subtract_exponential_fusion.4, f32[3,512,1536]{2,1,0:T(8,128)} %fusion.163, bf16[3,64,3072]{2,1,0:T(8,128)(2,1)} %get-tuple-element.602, s32[]{:T(128)S(6)} %select_n.98), kind=kOutput, calls=%fused_computation.31.clone.1 | convolution fusion | flops 314084352 | bytes 40304648 | tf_op jit(solution)/shard_map/while/body/eval_jaxpr/hqk,hdq->hdk/dot_general | solution.py:103
  765.3 15.4 %fusion.166 = bf16[6,3,64,512]{3,2,1,0:T(8,128)(2,1)} fusion(bf16[6,3,64,512]{3,2,1,0:T(8,128)(2,1)} %get-tuple-element.583, s32[]{:T(128)} %get-tuple-element.580, f32[3,512,1536]{2,1,0:T(8,128)} %subtract_exponential_fusion.4, f32[3,512,1536]{2,1,0:T(8,128)} %fusion.163, bf16[3,64,4096]{2,1,0:T(8,128)(2,1)} %get-tuple-element.605, s32[]{:T(128)S(6)} %select_n.97), kind=kOutput, calls=%fused_computation.34.clone.1 | convolution fusion | flops 313789440 | bytes 38732292 | tf_op jit(solution)/shard_map/while/body/eval_jaxpr/hqk,hdk->hdq/dot_general | solution.py:100
  780.7 6.1 fusion.165
  799.8 9.9 copy.164
  809.7 157.8 %all_to_all.51 = bf16[3,192,3072]{1,0,2:T(4,128)(2,1)} all-to-all(bf16[3,192,3072]{1,0,2:T(4,128)(2,1)} %copy.164), channel_id=1, replica_groups=mesh['seq'=8,'head'=4] {'head'}, dimensions={2} | all-to-all | bytes 7077888 | tf_op jit(solution)/shard_map/all_to_all | solution.py:281
  967.5 9.8 copy.166
  977.4 8.1 convolution_bitcast_fusion
  985.5 8.0 copy.178
  997.7 10.8 copy.176
  1017.8 41.1 %all-reduce.14 = (f32[768]{0:T(1024)}, f32[768]{0:T(1024)}, f32[768]{0:T(1024)}, f32[768]{0:T(1024)}, f32[768]{0:T(1024)}, /*index=5*/f32[3072]{0:T(1024)}, f32[...) all-reduce(f32[768]{0:T(1024)} %reduce_sum.241, ...), channel_id=3, replica_groups=mesh['seq'=8,'head'=4] {'seq','head'}, use_global_device_ids=true, to_apply=%region_22.23.clone | all-reduce | flops 12289 | bytes 98312
  1070.2 6.5 convolution_add_fusion
  1083.0 29.1 %reduce-scatter.17.cloned.1.call-done = f32[24,2304]{1,0:T(8,128)} async-done(((f32[768,2304]{1,0:T(8,128)}), f32[24,2304]{1,0:T(8,128)}) %reduce-scatter.17.cloned.1.call-update) | async-done | bytes 221200
  (305 shorter events, 211.6 us)
Async XLA Ops:
  7.2 2.0 copy-start
  19.5 6.7 copy-start.37
  19.5 111.4 %all-to-all-start = ((bf16[3,768,768]{2,0,1:T(4,128)(2,1)}), bf16[3,768,768]{2,0,1:T(4,128)(2,1)}, u32[]{:S(2)}, u32[]{:S(2)}) async-start(bf16[3,768,768]{2,0,1:T(4,128)(2,1)} %copy.151), calls=%async_computation | async-start | bytes 9437184 | tf_op jit(solution)/shard_map/all_to_all | solution.py:187
  155.4 5.4 copy-start.4
  168.0 1.3 copy-start.44
  177.9 4.8 copy-start.45
  182.8 1.2 copy-start.44
  192.7 4.8 copy-start.45
  197.5 1.2 copy-start.44
  207.5 4.8 copy-start.45
  212.3 1.2 copy-start.44
  222.3 4.8 copy-start.45
  227.1 1.2 copy-start.44
  237.1 4.8 copy-start.45
  241.9 1.2 copy-start.44
  251.9 4.8 copy-start.45
  266.0 32.3 %all-to-all-start.1 = ((bf16[192,4,768]{2,0,1:T(8,128)(2,1)}), bf16[192,4,768]{2,0,1:T(8,128)(2,1)}, u32[]{:S(2)}, u32[]{:S(2)}) async-start(bf16[192,4,768]{2,0,1:T(8,128)(2,1)} %copy.157), calls=%async_computation.1 | async-start | bytes 2359296 | tf_op jit(solution)/shard_map/all_to_all | solution.py:192
  270.2 28.1 %copy-start.40 = (f32[768]{0:T(1024)S(1)}, f32[768]{0:T(1024)}, u32[]{:S(2)}) copy-start(f32[768]{0:T(1024)} %param.32) | copy-start | bytes 9220
  270.3 812.8 %reduce-scatter.15.cloned.1.call-start = ((), (), s32[]{:S(2)}) async-start(), calls=%async_computation.12 | async-start | bytes 2433024 | tf_op jit(solution)/shard_map/reduce_scatter | solution.py:306
  275.1 18.6 %copy-start.19 = (s32[768]{0:T(1024)}, s32[768]{0:T(1024)S(1)}, u32[]{:S(2)}) copy-start(s32[768]{0:T(1024)S(1)} %iota_add_fusion) | copy-start | bytes 9220
  298.3 3.8 slice-start.2
  298.3 3.8 slice-start.3
  298.3 33.7 %slice-start = ((s8[4718592]{0:T(1024)(128)(4,1)}), s8[4194304]{0:T(1024)(128)(4,1)S(1)}, s32[]{:S(2)}) async-start(s8[4718592]{0:T(1024)(128)(4,1)} %bitcast.137), calls=%async_computation.14 | async-start | bytes 8388608
  301.7 30.3 %copy-start.5 = (f32[768,768]{0,1:T(8,128)}, f32[768,768]{0,1:T(8,128)S(1)}, u32[]{:S(2)}) copy-start(f32[768,768]{0,1:T(8,128)S(1)} %get-tuple-element.376) | copy-start | bytes 7077892
  301.7 1.6 copy-start.33
  301.7 1.7 copy-start.38
  301.7 1.7 copy-start.42
  301.8 30.3 %copy-start.17 = (f32[768]{0:T(1024)}, f32[768]{0:T(1024)S(1)}, u32[]{:S(2)}) copy-start(f32[768]{0:T(1024)S(1)} %broadcast_multiply_fusion.5) | copy-start | bytes 9220
  303.5 28.6 %copy-start.24 = (f32[768]{0:T(1024)}, f32[768]{0:T(1024)S(1)}, u32[]{:S(2)}) copy-start(f32[768]{0:T(1024)S(1)} %add_rsqrt_fusion.1) | copy-start | bytes 9220
  303.5 28.6 %slice-start.1 = ((s8[4718592]{0:T(1024)(128)(4,1)}), s8[524288]{0:T(1024)(128)(4,1)S(1)}, s32[]{:S(2)}) async-start(s8[4718592]{0:T(1024)(128)(4,1)} %bitcast.137), calls=%async_computation.15 | async-start | bytes 1048576
  303.5 28.6 %copy-start.41 = (f32[768]{0:T(1024)S(1)}, f32[768]{0:T(1024)}, u32[]{:S(2)}) copy-start(f32[768]{0:T(1024)} %param.38) | copy-start | bytes 9220
  332.0 4.7 copy-start.46
  336.7 1.5 copy-start.1
  337.1 1.1 copy-start.20
  337.5 1.7 copy-start.8
  337.5 1.7 copy-start.32
  337.5 2.0 copy-start.15
  337.5 2.6 copy-start.29
  337.5 2.6 copy-start.36
  339.2 4.8 copy-start.26
  339.7 1.3 copy-start.13
  339.7 1.3 copy-start.21
  339.8 1.3 copy-start.27
  352.1 730.9 %reduce-scatter.9.cloned.1.call-start = ((), (), s32[]{:S(2)}) async-start(), calls=%async_computation.9 | async-start | bytes 2433024 | tf_op jit(solution)/shard_map/reduce_scatter | solution.py:296
  352.7 4.6 copy-start.2
  357.4 1.5 copy-start.39
  357.4 16.9 %slice-start.4 = ((s8[4718592]{0:T(1024)(128)(4,1)}), s8[4194304]{0:T(1024)(128)(4,1)S(1)}, s32[]{:S(2)}) async-start(s8[4718592]{0:T(1024)(128)(4,1)} %bitcast.141), calls=%async_computation.18 | async-start | bytes 8388608
  358.9 15.4 %copy-start.10 = (f32[768,768]{0,1:T(8,128)}, f32[768,768]{0,1:T(8,128)S(1)}, u32[]{:S(2)}) copy-start(f32[768,768]{0,1:T(8,128)S(1)} %get-tuple-element.334) | copy-start | bytes 7077892
  358.9 15.4 %copy-start.6 = (f32[768,768]{0,1:T(8,128)S(1)}, f32[768,768]{0,1:T(8,128)}, u32[]{:S(2)}) copy-start(f32[768,768]{0,1:T(8,128)} %copy-done.5) | copy-start | bytes 7077892
  358.9 15.4 %copy-start.18 = (f32[768]{0:T(1024)S(1)}, f32[768]{0:T(1024)}, u32[]{:S(2)}) copy-start(f32[768]{0:T(1024)} %copy-done.17) | copy-start | bytes 9220
  358.9 15.4 %copy-start.25 = (f32[768]{0:T(1024)S(1)}, f32[768]{0:T(1024)}, u32[]{:S(2)}) copy-start(f32[768]{0:T(1024)} %copy-done.24) | copy-start | bytes 9220
  358.9 15.4 %copy-start.34 = (f32[768]{0:T(1024)S(1)}, f32[768]{0:T(1024)}, u32[]{:S(2)}) copy-start(f32[768]{0:T(1024)} %param.33) | copy-start | bytes 9220
  358.9 15.4 %slice-start.5 = ((s8[4718592]{0:T(1024)(128)(4,1)}), s8[524288]{0:T(1024)(128)(4,1)S(1)}, s32[]{:S(2)}) async-start(s8[4718592]{0:T(1024)(128)(4,1)} %bitcast.141), calls=%async_computation.19 | async-start | bytes 1048576
  383.3 1.4 copy-start.7
  388.6 694.4 %reduce-scatter.11.cloned.1.call-start = ((), (), s32[]{:S(2)}) async-start(), calls=%async_computation.10 | async-start | bytes 9732096 | tf_op jit(solution)/shard_map/reduce_scatter | solution.py:300
  404.3 37.2 %all-to-all-start.2 = ((bf16[4,192,768]{2,1,0:T(8,128)(2,1)}), bf16[4,192,768]{2,1,0:T(8,128)(2,1)}, u32[]{:S(2)}, u32[]{:S(2)}) async-start(bf16[4,192,768]{2,1,0:T(8,128)(2,1)} %pad_maximum_fusion.1), calls=%async_computation.2 | async-start | bytes 2359296 | tf_op jit(solution)/shard_map/all_to_all | solution.py:163
  408.6 674.4 %reduce-scatter.13.cloned.1.call-start = ((), (), s32[]{:S(2)}) async-start(), calls=%async_computation.11 | async-start | bytes 9732096 | tf_op jit(solution)/shard_map/reduce_scatter | solution.py:302
  419.5 692.6 %reduce-scatter.17.cloned.1.call-start = ((), (), s32[]{:S(2)}) async-start(), calls=%async_computation.13 | async-start | bytes 7299072
  794.0 3.8 copy-start.9
  993.5 2.4 copy-start.14
  993.5 2.4 copy-start.22
  993.6 2.4 copy-start.28
  993.6 2.4 copy-start.30
  1008.5 9.2 copy-start.23
  (7 other events, 5.0 us)
Sparse Core Ops, SparseCore 0:
  352.3 107.5 reduce-scatter.14
  465.7 98.6 reduce-scatter.8
  570.9 135.2 reduce-scatter.10
  712.5 149.1 reduce-scatter.12
  993.6 118.4 reduce-scatter.16
